TPU v7x, 256 devices: a whole 4x4x8 slice. The times are simulated.
256 devices in a mesh: ctx: 16 (over y, x), exp: 8 (over z), dp: 2 (over core).
Axes of the slice: x: 4, y: 4, z: 8, core: 2. Of those that a mesh axis runs over, the one named last changes fastest.
Arguments:
- residual: bfloat16 [2048, 4096], P('ctx', ('exp', 'dp')), may hold values from -6 to 6
- ssm_values: bfloat16 [2048, 4096], P('ctx', ('exp', 'dp')), may hold values from -6 to 6
- ssm_keys: bfloat16 [2048, 64], P('ctx'), may hold values from -6 to 6
- ssm_queries: bfloat16 [2048, 64], P('ctx'), may hold values from -0.015625 to 0.015625
- log_decay: float32 [2048, 64], P('ctx', ('exp', 'dp')), may hold values from -1 to 0, as said below
- expert_ids: int32 [2048, 2], P('ctx'), may hold values from 0 to 7, all different within a row; in each aligned block of 128 rows (0 to 127, 128 to 255, ...) at most 40 rows name the same one
- gate_probs: float32 [2048, 2], P('ctx'), may hold values from 0.2 to 1
- norm_gain: float32 [4096], P(('exp', 'dp')), may hold values from 0.5 to 1.5
- w_gate: bfloat16 [8, 4096, 8192], P('exp', None, ('ctx', 'dp')), may hold values from -0.09375 to 0.09375
- w_up: bfloat16 [8, 4096, 8192], P('exp', None, ('ctx', 'dp')), may hold values from -0.09375 to 0.09375
- w_down: bfloat16 [8, 4096, 8192], P('exp', None, ('ctx', 'dp')), may hold values from -0.0625 to 0.0625
- out_grad: bfloat16 [2048, 4096], P('ctx', ('exp', 'dp')), may hold values from -6 to 6
Outputs:
- grad_residual: bfloat16 [2048, 4096], P('ctx', ('exp', 'dp'))
- grad_values: bfloat16 [2048, 4096], P('ctx', ('exp', 'dp'))
- grad_keys: float32 [2048, 64], P('ctx')
- grad_queries: float32 [2048, 64], P('ctx')
- grad_decay: float32 [2048, 64], P('ctx', ('exp', 'dp'))
- grad_probs: float32 [2048, 2], P('ctx')
- grad_gain: float32 [4096], P(('exp', 'dp'))
- w_gate_grad: bfloat16 [8, 4096, 8192], P('exp', None, ('ctx', 'dp'))
- w_up_grad: bfloat16 [8, 4096, 8192], P('exp', None, ('ctx', 'dp'))
- w_down_grad: bfloat16 [8, 4096, 8192], P('exp', None, ('ctx', 'dp'))
Inputs may be any that keep to these rules, and one draw needn't show every extreme that they name: `expert_ids`: each token names two different experts; among the 128 tokens of one index of ctx (aligned blocks) no expert is named more than 40 times, a bound that some block reaches. `log_decay`: negative everywhere.
All inputs are finite; a program needn't handle non-finite values.
Results may differ from a plain program's by a relative error of at most 0.028.
Values may be sent and summed in bfloat16 or wider, within the bound.
No kernel may reach another device: no remote copies, remote signals or barrier semaphores. Data moves between devices by JAX's collectives and lax.ppermute only.
A program may use at most 128 MiB of HBM per device.

v0:
```python
import jax
import jax.numpy as jnp
from jax import lax
from jax.sharding import PartitionSpec as P

HIGH = lax.Precision.HIGHEST
EPS = 1e-05


def entering(x, axis, join, neutral):
    place = lax.axis_index(axis)
    gathered = jax.tree.map(
        lambda a, kind: lax.all_gather(a.astype(kind), axis), x, (jnp.bfloat16, jnp.bfloat16)
    )
    state = jax.tree.map(lambda a, e: jnp.zeros_like(a) + jnp.asarray(e, a.dtype), x, neutral)

    def entering_one(step, state):
        return join(
            state,
            jax.tree.map(
                lambda a, own: lax.dynamic_index_in_dim(a, step, 0, False).astype(own.dtype),
                gathered,
                x,
            ),
        )

    return lax.fori_loop(0, place, entering_one, state)


def carried_in(x, axis, join, neutral):
    count = lax.axis_size(axis)
    place = lax.axis_index(axis)
    ahead = count - 1 - place
    gathered = jax.tree.map(
        lambda a, kind: lax.all_gather(a.astype(kind), axis),
        x,
        jax.tree.map(lambda a: jnp.bfloat16 if a.dtype == jnp.float32 else a.dtype, x),
    )
    state = jax.tree.map(lambda a, e: jnp.zeros_like(a) + jnp.asarray(e, a.dtype), x, neutral)

    def carried_one(step, state):
        source = count - 1 - step
        return join(
            state,
            jax.tree.map(
                lambda a, own: lax.dynamic_index_in_dim(a, source, 0, False).astype(own.dtype),
                gathered,
                x,
            ),
        )

    return lax.fori_loop(0, ahead, carried_one, state)


def block_state(values, key_rows, log_decay):
    cumulative = jnp.cumsum(log_decay, axis=0)
    total_log = cumulative[-1]
    tail_decay = jnp.exp(total_log[None, :] - cumulative)
    weighted = tail_decay[:, :, None] * values
    state_local = jnp.einsum("shp,sn->hpn", weighted, key_rows, precision=HIGH)
    return (jnp.exp(total_log), state_local)


def block_output(values, key_rows, queries, log_decay, state_in):
    cumulative = jnp.cumsum(log_decay, axis=0)
    length = values.shape[0]
    row_index = lax.broadcasted_iota(jnp.int32, (length, length), 0)
    col_index = lax.broadcasted_iota(jnp.int32, (length, length), 1)
    causal = (row_index >= col_index)[None]
    cum_heads = cumulative.T
    log_gap = jnp.where(causal, cum_heads[:, :, None] - cum_heads[:, None, :], 0.0)
    decay_mat = jnp.where(causal, jnp.exp(log_gap), 0.0)
    scores = jnp.dot(queries, key_rows.T, precision=HIGH)
    inner_part = jnp.einsum("hts,shp->thp", decay_mat * scores[None], values, precision=HIGH)
    carried = jnp.einsum("tn,hpn->thp", queries, state_in, precision=HIGH)
    return inner_part + jnp.exp(cumulative)[:, :, None] * carried


def silu_parts(gate_act):
    sigmoid_val = jax.nn.sigmoid(gate_act)
    return (gate_act * sigmoid_val, sigmoid_val * (1.0 + gate_act * (1.0 - sigmoid_val)))


def route_slots(token_ids, expert_count):
    owners = token_ids.reshape(-1)
    onehot = (owners[:, None] == jnp.arange(expert_count, dtype=jnp.int32)[None, :]).astype(
        jnp.int32
    )
    rank_before = jnp.cumsum(onehot, axis=0) - onehot
    return (owners, jnp.sum(rank_before * onehot, axis=1))


def combine_states(earlier_part, later_part):
    return (
        earlier_part[0] * later_part[0],
        later_part[0][:, None, None] * earlier_part[1] + later_part[1],
    )


def arrange_rows(gathered, ctx_count, dp_count):
    capacity = gathered.shape[1]
    exp_count = gathered.shape[2]
    feat = gathered.shape[3]
    shaped = gathered.reshape(ctx_count, dp_count, capacity, exp_count, feat)
    return shaped.transpose(0, 2, 3, 1, 4).reshape(
        ctx_count * capacity, exp_count * dp_count * feat
    )


def arrange_sums(full_term, ctx_count, dp_count, exp_count, capacity):
    feat = full_term.shape[1] // (exp_count * dp_count)
    shaped = full_term.reshape(ctx_count, capacity, exp_count, dp_count, feat)
    return shaped.transpose(0, 3, 1, 2, 4).reshape(
        ctx_count * dp_count * capacity, exp_count * feat
    )


def per_device(
    residual,
    ssm_values,
    ssm_keys,
    ssm_queries,
    log_decay,
    expert_ids,
    gate_probs,
    norm_gain,
    w_gate,
    w_up,
    w_down,
    out_grad,
):
    tokens = residual.shape[0]
    feat = residual.shape[1]
    heads_here = log_decay.shape[1]
    head_size = feat // heads_here
    model_width = w_gate.shape[1]
    ctx_count = lax.axis_size("ctx")
    exp_count = lax.axis_size("exp")
    dp_count = lax.axis_size("dp")
    expert_count = w_gate.shape[0] * exp_count
    capacity = 5 * tokens // (2 * expert_count)
    block_vals = ssm_values.astype(jnp.float32).reshape(tokens, heads_here, head_size)
    block_keys = ssm_keys.astype(jnp.float32)
    block_queries = ssm_queries.astype(jnp.float32)
    (decay_total, state_local), state_pull = jax.vjp(block_state, block_vals, block_keys, log_decay)
    neutral = (jnp.ones_like(decay_total), jnp.zeros_like(state_local))
    state_in = entering((decay_total, state_local), "ctx", combine_states, neutral)[1]
    mixer_out, output_pull = jax.vjp(
        block_output, block_vals, block_keys, block_queries, log_decay, state_in
    )
    hidden = (residual.astype(jnp.float32) + mixer_out.reshape(tokens, feat)).astype(jnp.bfloat16)
    hidden_f = hidden.astype(jnp.float32)
    square_sum = lax.psum(jnp.sum(hidden_f * hidden_f, axis=1), ("exp", "dp"))
    inv_rms = lax.rsqrt(square_sum / model_width + EPS)[:, None]
    normed = (hidden_f * inv_rms * norm_gain[None, :]).astype(jnp.bfloat16)
    owners, slot_index = route_slots(expert_ids, expert_count)
    pair_rows = jnp.repeat(normed, 2, axis=0)
    dout_rows = jnp.repeat(out_grad, 2, axis=0)
    pair_prob = gate_probs.reshape(-1)
    pair_cot = (pair_prob[:, None] * dout_rows.astype(jnp.float32)).astype(jnp.bfloat16)
    empty = jnp.zeros((expert_count, capacity, feat), jnp.bfloat16)
    send_rows = empty.at[owners, slot_index].set(pair_rows).reshape(expert_count, capacity, 1, feat)
    got_rows = lax.all_to_all(send_rows, "exp", split_axis=0, concat_axis=2, tiled=True)
    all_rows = lax.all_gather(got_rows, ("ctx", "dp"), axis=0, tiled=True)
    rows_flat = arrange_rows(all_rows, ctx_count, dp_count)
    act_gate = jnp.dot(rows_flat, w_gate[0], preferred_element_type=jnp.float32)
    act_up = jnp.dot(rows_flat, w_up[0], preferred_element_type=jnp.float32)
    swish_val, swish_slope = silu_parts(act_gate)
    hidden_act = (swish_val * act_up).astype(jnp.bfloat16)
    full_out = lax.dot_general(
        hidden_act, w_down[0], (((1,), (1,)), ((), ())), preferred_element_type=jnp.float32
    )
    out_total = lax.psum_scatter(
        arrange_sums(full_out, ctx_count, dp_count, exp_count, capacity).astype(jnp.bfloat16),
        ("ctx", "dp"),
        scatter_dimension=0,
        tiled=True,
    )
    expert_out = out_total.reshape(1, capacity, exp_count, feat)
    back_out = lax.all_to_all(expert_out, "exp", split_axis=2, concat_axis=0, tiled=True).reshape(
        expert_count, capacity, feat
    )
    out_pairs = back_out[owners, slot_index]
    probs_part = jnp.einsum(
        "kd,kd->k", out_pairs, dout_rows, preferred_element_type=jnp.float32
    ).reshape(tokens, 2)
    grad_probs = lax.psum(probs_part, ("exp", "dp"))
    send_cot = empty.at[owners, slot_index].set(pair_cot).reshape(expert_count, capacity, 1, feat)
    got_cot = lax.all_to_all(send_cot, "exp", split_axis=0, concat_axis=2, tiled=True)
    all_cot = lax.all_gather(got_cot, ("ctx", "dp"), axis=0, tiled=True)
    cot_flat = arrange_rows(all_cot, ctx_count, dp_count)
    grad_act = jnp.dot(cot_flat, w_down[0], preferred_element_type=jnp.float32)
    grad_gate = (grad_act * act_up * swish_slope).astype(jnp.bfloat16)
    grad_up = (grad_act * swish_val).astype(jnp.bfloat16)
    full_back = lax.dot_general(
        grad_gate, w_gate[0], (((1,), (1,)), ((), ())), preferred_element_type=jnp.float32
    ) + lax.dot_general(
        grad_up, w_up[0], (((1,), (1,)), ((), ())), preferred_element_type=jnp.float32
    )
    back_total = lax.psum_scatter(
        arrange_sums(full_back, ctx_count, dp_count, exp_count, capacity).astype(jnp.bfloat16),
        ("ctx", "dp"),
        scatter_dimension=0,
        tiled=True,
    )
    pair_back = back_total.reshape(1, capacity, exp_count, feat)
    back_in = lax.all_to_all(pair_back, "exp", split_axis=2, concat_axis=0, tiled=True).reshape(
        expert_count, capacity, feat
    )
    grad_normed = (
        back_in[owners, slot_index].astype(jnp.float32).reshape(tokens, 2, feat).sum(axis=1)
    )
    w_gate_grad = jnp.dot(rows_flat.T, grad_gate, preferred_element_type=jnp.float32).astype(
        jnp.bfloat16
    )[None]
    w_up_grad = jnp.dot(rows_flat.T, grad_up, preferred_element_type=jnp.float32).astype(
        jnp.bfloat16
    )[None]
    w_down_grad = jnp.dot(cot_flat.T, hidden_act, preferred_element_type=jnp.float32).astype(
        jnp.bfloat16
    )[None]
    scaled = grad_normed * norm_gain[None, :]
    inner_sum = lax.psum(jnp.sum(hidden_f * scaled, axis=1), ("exp", "dp"))
    projection = (inner_sum / model_width)[:, None]
    grad_hidden = (
        out_grad.astype(jnp.float32) + inv_rms * scaled - hidden_f * inv_rms**3 * projection
    )
    gain_part = jnp.sum(grad_normed * hidden_f * inv_rms, axis=0)
    grad_gain = lax.psum(gain_part, "ctx")
    grad_mixer = grad_hidden.reshape(tokens, heads_here, head_size)
    vals_first, keys_first, queries_part, decay_first, carry_cot = output_pull(grad_mixer)
    grad_state = carried_in((decay_total, carry_cot), "ctx", combine_states, neutral)[1]
    grad_total = jnp.sum(grad_state * state_in, axis=(1, 2))
    vals_second, keys_second, decay_second = state_pull((grad_total, grad_state))
    grad_keys, grad_queries = (
        lax.psum((keys_first + keys_second).astype(jnp.bfloat16), ("exp", "dp")).astype(
            jnp.float32
        ),
        lax.psum(queries_part.astype(jnp.bfloat16), ("exp", "dp")).astype(jnp.float32),
    )
    grad_residual = grad_hidden.astype(jnp.bfloat16)
    grad_values = (vals_first + vals_second).reshape(tokens, feat).astype(jnp.bfloat16)
    grad_decay = decay_first + decay_second
    return (
        grad_residual,
        grad_values,
        grad_keys,
        grad_queries,
        grad_decay,
        grad_probs,
        grad_gain,
        w_gate_grad,
        w_up_grad,
        w_down_grad,
    )


def solution(mesh):
    return jax.shard_map(
        per_device,
        mesh=mesh,
        in_specs=(
            P("ctx", ("exp", "dp")),
            P("ctx", ("exp", "dp")),
            P("ctx", None),
            P("ctx", None),
            P("ctx", ("exp", "dp")),
            P("ctx", None),
            P("ctx", None),
            P(("exp", "dp")),
            P("exp", None, ("ctx", "dp")),
            P("exp", None, ("ctx", "dp")),
            P("exp", None, ("ctx", "dp")),
            P("ctx", ("exp", "dp")),
        ),
        out_specs=(
            P("ctx", ("exp", "dp")),
            P("ctx", ("exp", "dp")),
            P("ctx", None),
            P("ctx", None),
            P("ctx", ("exp", "dp")),
            P("ctx", None),
            P(("exp", "dp")),
            P("exp", None, ("ctx", "dp")),
            P("exp", None, ("ctx", "dp")),
            P("exp", None, ("ctx", "dp")),
        ),
        check_vma=False,
    )
```

profile of v0, /device:TPU:2, one launch (start us, length us, event | category | flops | bytes accessed | tf_op | source)
XLA Modules:
  0.0 650.5 jit_solution(5369685150378966095)
XLA Ops:
  7.3 0.9 copy.158
  9.5 0.8 copy.161
  10.4 0.9 broadcast_in_dim.74
  11.6 13.2 %scatter_fusion = bf16[8,40,256]{2,1,0:T(8,128)(2,1)S(1)} fusion(bf16[8,40,256]{2,1,0:T(8,128)(2,1)S(1)} %broadcast_in_dim.73.clone.1, s32[256]{0:T(256)S(1)} %bitcast.193, bf16[256,256]{1,0:T(8,128)(2,1)S(1)} %fusion.19), kind=kCustom, calls=%fused_computation.2 | custom fusion | bytes 395264 | tf_op jit(solution)/shard_map/scatter | solution.py:188
  24.9 18.0 %all_to_all.66 = bf16[8,40,1,256]{3,1,2,0:T(8,128)(2,1)S(1)} all-to-all(bf16[8,40,1,256]{3,1,2,0:T(8,128)(2,1)S(1)} %bitcast.200), channel_id=1, replica_groups=mesh['ctx'=16,'exp'=8,'dp'=2] {'exp'}, dimensions={0} | all-to-all | bytes 327680 | tf_op jit(solution)/shard_map/all_to_all | solution.py:189
  44.6 20.7 %all-gather.4 = bf16[16,1,4]{2,1,0:T(2,128)(2,1)S(1)} all-gather(bf16[1,1,4]{2,1,0:T(2,128)(2,1)S(1)} %get-tuple-element.299), channel_id=1, replica_groups=mesh['ctx'=16,'exp'=8,'dp'=2] {'ctx'}, dimensions={0}, use_global_device_ids=true | all-gather | bytes 136 | tf_op jit(solution)/shard_map/all_gather | solution.py:13
  65.4 1.0 copy.152
  67.0 27.6 %all-gather = bf16[64,64,64]{2,1,0:T(8,128)(2,1)} all-gather(bf16[4,64,64]{2,1,0:T(8,128)(2,1)S(1)} %convolution_convert_fusion.4), channel_id=2, replica_groups=mesh['ctx'=16,'exp'=8,'dp'=2] {'ctx'}, dimensions={0}, use_global_device_ids=true | all-gather | bytes 557056 | tf_op jit(solution)/shard_map/all_gather | solution.py:13
  94.8 1.0 while.26
  94.9 0.9 convert_add_fusion.4
  96.7 23.5 %psum.42 = f32[128]{0:T(128)S(1)} all-reduce(f32[128]{0:T(128)S(1)} %get-tuple-element.291), channel_id=1, replica_groups=mesh['ctx'=16,'exp'=8,'dp'=2] {'exp','dp'}, use_global_device_ids=true, to_apply=%region_4.5 | all-reduce | flops 128 | bytes 1024 | tf_op jit(solution)/shard_map/psum | solution.py:153
  121.1 13.2 %scatter_fusion.1 = bf16[8,40,256]{2,1,0:T(8,128)(2,1)S(1)} fusion(bf16[8,40,256]{2,1,0:T(8,128)(2,1)S(1)} %broadcast_in_dim.73.clone, s32[256]{0:T(256)S(1)} %bitcast.194, bf16[256,256]{1,0:T(8,128)(2,1)S(1)} %reshape.273), kind=kCustom, calls=%fused_computation.3 | custom fusion | bytes 395264 | tf_op jit(solution)/shard_map/scatter | solution.py:162
  134.3 12.5 %all_to_all.67 = bf16[8,40,1,256]{3,1,2,0:T(8,128)(2,1)S(1)} all-to-all(bf16[8,40,1,256]{3,1,2,0:T(8,128)(2,1)S(1)} %bitcast.199), channel_id=1, replica_groups=mesh['ctx'=16,'exp'=8,'dp'=2] {'exp'}, dimensions={0} | all-to-all | bytes 327680 | tf_op jit(solution)/shard_map/all_to_all | solution.py:163
  148.1 13.0 %copy.164 = bf16[16,40,8,2,256]{4,3,2,1,0:T(2,128)(2,1)} copy(bf16[16,40,8,2,256]{4,2,1,3,0:T(8,128)(2,1)} %bitcast.203) | data formatting | bytes 10485760 | tf_op jit(solution)/shard_map/transpose | solution.py:105
  161.1 9.6 %reshape.236 = bf16[640,4096]{1,0:T(8,128)(2,1)} reshape(bf16[16,40,8,2,256]{4,3,2,1,0:T(2,128)(2,1)} %copy.164) | data formatting | bytes 10485760 | tf_op jit(solution)/shard_map/reshape | solution.py:105
  170.7 35.8 %all-gather.10.cloned.1.call-done = bf16[32,40,8,1,256]{4,2,3,1,0:T(8,128)(2,1)} async-done(((bf16[1,40,8,1,256]{4,2,3,1,0:T(8,128)(2,1)}), bf16[32,40,8,1,256]{4,2,3,1,0:T(8,128)(2,1)}) %all-gather.10.cloned.1.call-update) | async-done | bytes 5242896 | tf_op jit(solution)/shard_map/all_gather | solution.py:164
  206.6 13.0 %copy.167 = bf16[16,40,8,2,256]{4,3,2,1,0:T(2,128)(2,1)} copy(bf16[16,40,8,2,256]{4,2,1,3,0:T(8,128)(2,1)} %bitcast.204) | data formatting | bytes 10485760 | tf_op jit(solution)/shard_map/transpose | solution.py:105
  219.6 9.6 %reshape.240 = bf16[640,4096]{1,0:T(8,128)(2,1)} reshape(bf16[16,40,8,2,256]{4,3,2,1,0:T(2,128)(2,1)} %copy.167) | data formatting | bytes 10485760 | tf_op jit(solution)/shard_map/reshape | solution.py:105
  229.2 4.2 fusion.10
  233.9 1.5 fusion.5
  235.5 2.4 multiply_convert_fusion
  238.0 1.6 convert_bitcast_fusion
  239.6 2.3 copy.176
  241.9 4.6 copy.191
  247.0 1.1 copy-done.4
  248.2 1.6 fusion.3
  249.8 3.8 add_convert_fusion
  253.6 9.6 %convert_element_type.165 = bf16[16,40,8,2,256]{4,3,2,1,0:T(2,128)(2,1)} reshape(bf16[640,4096]{1,0:T(8,128)(2,1)} %add_convert_fusion) | data formatting | bytes 10485760 | tf_op jit(solution)/shard_map/convert_element_type | solution.py:201
  263.2 3.6 copy.168
  266.8 4.5 copy.189
  271.3 1.0 copy-done.10
  272.3 5.9 fusion.2
  278.2 60.3 %reduce-scatter.5.cloned.1.call-done = bf16[40,2048]{1,0:T(8,128)(2,1)} async-done(((bf16[1280,2048]{1,0:T(8,128)(2,1)}), bf16[40,2048]{1,0:T(8,128)(2,1)}) %reduce-scatter.5.cloned.1.call-update) | async-done | bytes 163856 | tf_op jit(solution)/shard_map/reduce_scatter | solution.py:173
  338.5 0.9 copy.192
  340.1 7.0 %all-to-all-start.3 = ((bf16[1,40,8,256]{3,1,0,2:T(8,128)(2,1)}), bf16[1,40,8,256]{3,1,0,2:T(8,128)(2,1)S(1)}, u32[]{:S(2)}, u32[]{:S(2)}) async-start(bf16[1,40,8,256]{3,1,0,2:T(8,128)(2,1)} %copy.177), calls=%async_computation.5 | async-start | bytes 327680 | tf_op jit(solution)/shard_map/all_to_all | solution.py:180
  347.2 5.7 fusion
  352.9 81.2 %reduce-scatter.3.cloned.1.call-done = bf16[40,2048]{1,0:T(8,128)(2,1)} async-done(((bf16[1280,2048]{1,0:T(8,128)(2,1)}), bf16[40,2048]{1,0:T(8,128)(2,1)}) %reduce-scatter.3.cloned.1.call-update) | async-done | bytes 163856 | tf_op jit(solution)/shard_map/reduce_scatter | solution.py:200
  434.1 0.9 copy.190
  435.8 7.2 %all-to-all-start.2 = ((bf16[1,40,8,256]{3,1,0,2:T(8,128)(2,1)}), bf16[1,40,8,256]{3,1,0,2:T(8,128)(2,1)S(1)}, u32[]{:S(2)}, u32[]{:S(2)}) async-start(bf16[1,40,8,256]{3,1,0,2:T(8,128)(2,1)} %copy.169), calls=%async_computation.3 | async-start | bytes 327680 | tf_op jit(solution)/shard_map/all_to_all | solution.py:207
  443.0 5.7 fusion.1
  448.7 1.7 gather_fusion.1
  450.6 1.7 all-to-all-done.2
  452.4 1.7 gather_fusion
  454.6 46.5 %all-reduce.1 = (f32[128]{0:T(128)S(1)}, f32[128,2]{1,0:T(8,128)S(1)}) all-reduce(f32[128]{0:T(128)S(1)} %get-tuple-element.264, f32[128,2]{1,0:T(8,128)S(1)} %reshape.247), channel_id=1, replica_groups=mesh['ctx'=16,'exp'=8,'dp'=2] {'exp','dp'}, use_global_device_ids=true, to_apply=%region_13.14 | all-reduce | flops 384 | bytes 3072 | tf_op jit(solution)/shard_map/psum | solution.py:223
  502.6 25.1 %all-gather.3 = bf16[64,64,64]{2,1,0:T(8,128)(2,1)} all-gather(bf16[4,64,64]{2,1,0:T(8,128)(2,1)S(1)} %convolution_convert_fusion.3), channel_id=5, replica_groups=mesh['ctx'=16,'exp'=8,'dp'=2] {'ctx'}, dimensions={0}, use_global_device_ids=true | all-gather | bytes 557056 | tf_op jit(solution)/shard_map/all_gather | solution.py:35
  527.7 22.9 %while.27 = (s32[]{:T(128)}, f32[4,64,64]{2,1,0:T(8,128)S(1)}, s32[]{:T(128)}, bf16[16,4]{1,0:T(8,128)(2,1)}, bf16[16,4,64,64]{3,2,1,0:T(8,128)(2,1)}, /*index=5*/s32[]{:T(128)}, s32[]{:T(128)}, s32[]{:T(128)}, s32[]{:T(128)}) while((s32[]{:T(128)}, f32[4,64,64]{2,1,0:T(8,128)S(1)}, s32[]{:T(128)}, bf16[16,4]{1,0:T(8,128)(2,1)}, ...), condition=%wide.region_15.16_spmd, body=%wide.region_14.15_spmd.sunk | while | flops 49162 | bytes 164035 | solution.py:52
  528.4 0.9 convert_add_fusion.5
  530.0 0.9 convert_add_fusion.5
  531.7 0.9 convert_add_fusion.5
  533.3 0.9 convert_add_fusion.5
  534.9 0.9 convert_add_fusion.5
  536.6 0.9 convert_add_fusion.5
  538.2 0.9 convert_add_fusion.5
  539.8 0.9 convert_add_fusion.5
  541.5 0.9 convert_add_fusion.5
  543.1 0.9 convert_add_fusion.5
  544.8 0.9 convert_add_fusion.5
  546.4 0.9 convert_add_fusion.5
  548.0 0.9 convert_add_fusion.5
  549.7 0.9 convert_add_fusion.5
  550.9 39.5 %psum.47 = f32[256]{0:T(256)} all-reduce(f32[256]{0:T(256)S(1)} %get-tuple-element.263), channel_id=1, replica_groups=mesh['ctx'=16,'exp'=8,'dp'=2] {'ctx'}, use_global_device_ids=true, to_apply=%region_30.31 | all-reduce | flops 256 | bytes 2048 | tf_op jit(solution)/shard_map/psum | solution.py:229
  593.7 45.7 %all-reduce.2 = (bf16[128,64]{0,1:T(8,128)(2,1)S(1)}, bf16[128,64]{0,1:T(8,128)(2,1)S(1)}) all-reduce(bf16[128,64]{0,1:T(8,128)(2,1)S(1)} %fusion.16, bf16[128,64]{0,1:T(8,128)(2,1)S(1)} %fusion.17), channel_id=1, replica_groups=mesh['ctx'=16,'exp'=8,'dp'=2] {'exp','dp'}, use_global_device_ids=true, to_apply=%region_17.18 | all-reduce | flops 16384 | bytes 65536 | tf_op jit(solution)/shard_map/psum | solution.py:236
  640.8 1.1 reduce_window_sum.47
  641.9 1.1 reduce_window_sum.48
  (139 shorter events, 27.4 us)
Async XLA Ops:
  7.2 222.0 %copy-start = (bf16[1,4096,256]{2,1,0:T(8,128)(2,1)S(1)}, bf16[1,4096,256]{2,1,0:T(8,128)(2,1)}, u32[]{:S(2)}) copy-start(bf16[1,4096,256]{2,1,0:T(8,128)(2,1)} %param.26) | copy-start | bytes 6291460
  7.2 59.6 %copy-start.13 = (bf16[128,64]{0,1:T(8,128)(2,1)S(1)}, bf16[128,64]{0,1:T(8,128)(2,1)}, u32[]{:S(2)}) copy-start(bf16[128,64]{0,1:T(8,128)(2,1)} %param.18) | copy-start | bytes 49156
  7.2 87.4 %copy-start.12 = (bf16[128,64]{0,1:T(8,128)(2,1)S(1)}, bf16[128,64]{0,1:T(8,128)(2,1)}, u32[]{:S(2)}) copy-start(bf16[128,64]{0,1:T(8,128)(2,1)} %param.19) | copy-start | bytes 49156
  7.2 89.4 %copy-start.16 = (bf16[128,256]{1,0:T(8,128)(2,1)S(1)}, bf16[128,256]{1,0:T(8,128)(2,1)}, u32[]{:S(2)}) copy-start(bf16[128,256]{1,0:T(8,128)(2,1)} %param.16) | copy-start | bytes 196612
  7.2 113.6 %copy-start.17 = (f32[256]{0:T(256)S(1)}, f32[256]{0:T(256)}, u32[]{:S(2)}) copy-start(f32[256]{0:T(256)} %param.23) | copy-start | bytes 3076
  7.2 140.9 %all-gather.8.cloned.1.call-start = ((), (), s32[]{:S(2)}) async-start(), calls=%async_computation.8 | async-start | bytes 5406720 | tf_op jit(solution)/shard_map/all_gather | solution.py:190
  43.6 163.0 %all-gather.10.cloned.1.call-start = ((), (), s32[]{:S(2)}) async-start(), calls=%async_computation.9 | async-start | bytes 5406720 | tf_op jit(solution)/shard_map/all_gather | solution.py:164
  66.4 67.9 %copy-start.19 = (f32[4,128]{1,0:T(4,128)}, f32[4,128]{1,0:T(4,128)S(1)}, u32[]{:S(2)}) copy-start(f32[4,128]{1,0:T(4,128)S(1)} %copy.150) | copy-start | bytes 6148
  94.8 39.5 %copy-start.14 = (f32[128,128]{1,0:T(8,128)}, f32[128,128]{1,0:T(8,128)S(1)}, u32[]{:S(2)}) copy-start(f32[128,128]{1,0:T(8,128)S(1)} %fusion.65) | copy-start | bytes 196612
  95.8 38.5 %copy-start.18 = (bf16[16,4]{1,0:T(8,128)(2,1)}, bf16[16,4]{1,0:T(8,128)(2,1)S(1)}, u32[]{:S(2)}) copy-start(bf16[16,4]{1,0:T(8,128)(2,1)S(1)} %get-tuple-element.437) | copy-start | bytes 388
  147.5 191.0 %reduce-scatter.5.cloned.1.call-start = ((), (), s32[]{:S(2)}) async-start(), calls=%async_computation.7 | async-start | bytes 5406720 | tf_op jit(solution)/shard_map/reduce_scatter | solution.py:173
  229.2 4.2 copy-start.2
  229.2 4.7 copy-start.3
  233.9 1.6 copy-start.5
  238.0 3.9 copy-start.9
  246.6 1.6 copy-start.4
  246.6 187.5 %reduce-scatter.3.cloned.1.call-start = ((), (), s32[]{:S(2)}) async-start(), calls=%async_computation.6 | async-start | bytes 5406720 | tf_op jit(solution)/shard_map/reduce_scatter | solution.py:200
  248.2 1.6 copy-start.6
  248.2 1.6 copy-start.7
  271.3 1.0 copy-start.10
  340.1 95.7 %all-to-all-start.3 = ((bf16[1,40,8,256]{3,1,0,2:T(8,128)(2,1)}), bf16[1,40,8,256]{3,1,0,2:T(8,128)(2,1)S(1)}, u32[]{:S(2)}, u32[]{:S(2)}) async-start(bf16[1,40,8,256]{3,1,0,2:T(8,128)(2,1)} %copy.177), calls=%async_computation.5 | async-start | bytes 327680 | tf_op jit(solution)/shard_map/all_to_all | solution.py:180
  347.2 95.8 %copy-start.8 = (bf16[640,256]{1,0:T(8,128)(2,1)S(1)}, bf16[640,256]{1,0:T(8,128)(2,1)}, u32[]{:S(2)}) copy-start(bf16[640,256]{1,0:T(8,128)(2,1)} %get-tuple-element.297) | copy-start | bytes 983044
  435.8 16.6 %all-to-all-start.2 = ((bf16[1,40,8,256]{3,1,0,2:T(8,128)(2,1)}), bf16[1,40,8,256]{3,1,0,2:T(8,128)(2,1)S(1)}, u32[]{:S(2)}, u32[]{:S(2)}) async-start(bf16[1,40,8,256]{3,1,0,2:T(8,128)(2,1)} %copy.169), calls=%async_computation.3 | async-start | bytes 327680 | tf_op jit(solution)/shard_map/all_to_all | solution.py:207
  443.0 58.1 %copy-start.11 = (bf16[128,256]{1,0:T(8,128)(2,1)S(1)}, bf16[128,256]{1,0:T(8,128)(2,1)}, u32[]{:S(2)}) copy-start(bf16[128,256]{1,0:T(8,128)(2,1)} %param.27) | copy-start | bytes 196612
  443.0 58.1 %copy-start.21 = (f32[128]{0:T(128)S(1)}, f32[128]{0:T(128)}, u32[]{:S(2)}) copy-start(f32[128]{0:T(128)} %get-tuple-element.300) | copy-start | bytes 1540
  448.7 142.3 %copy-start.15 = (f32[128,128]{1,0:T(8,128)S(1)}, f32[128,128]{1,0:T(8,128)}, u32[]{:S(2)}) copy-start(f32[128,128]{1,0:T(8,128)} %copy-done.14) | copy-start | bytes 196612
  448.7 142.3 %copy-start.20 = (f32[4,128]{1,0:T(4,128)S(1)}, f32[4,128]{1,0:T(4,128)}, u32[]{:S(2)}) copy-start(f32[4,128]{1,0:T(4,128)} %copy-done.19) | copy-start | bytes 6148
  452.4 191.4 %copy-start.1 = (bf16[1,4096,256]{2,1,0:T(8,128)(2,1)S(1)}, bf16[1,4096,256]{2,1,0:T(8,128)(2,1)}, u32[]{:S(2)}) copy-start(bf16[1,4096,256]{2,1,0:T(8,128)(2,1)} %param.26) | copy-start | bytes 6291460
Sparse Core Ops, SparseCore 0:
  43.7 49.1 all-gather.7
  147.6 58.8 all-gather.9
  246.7 91.7 reduce-scatter.4
  342.4 91.7 reduce-scatter.2
where the time goes:
time: 657 us; the launch traced here: 650 us
  blocking collectives  259 us (39%)
  waiting for transfers between devices  179 us (27%)
  local copies, waits for them, and re-layouts  116 us (18%)
  matrix products  35.9 us (5%)
  other arithmetic  30.4 us (5%)
  starting transfers between devices  15.3 us (2%)
  between operations  14.5 us (2%)
    reduce_scatter x1, waiting for transfers between devices, per_device(): lax.psum_scatter(arrange_sums(full_back, ctx_count, dp_count, exp_count,...  81.2 us
    reduce_scatter x1, waiting for transfers between devices, per_device(): lax.psum_scatter(arrange_sums(full_out, ctx_count, dp_count, exp_count, c...  60.3 us
    all_gather x2, blocking collectives, entering(): lax.all_gather(a.astype(kind), axis)  48.3 us
    psum x1, blocking collectives, per_device(): inner_sum = lax.psum(jnp.sum(hidden_f * scaled, axis=1), ('exp', 'dp'))  46.5 us
    psum x1, blocking collectives, per_device(): lax.psum((keys_first + keys_second).astype(jnp.bfloat16), ('exp', 'dp'))  45.7 us
    psum x1, blocking collectives, per_device(): grad_gain = lax.psum(gain_part, 'ctx')  39.5 us
    all_gather x1, waiting for transfers between devices, per_device(): all_rows = lax.all_gather(got_rows, ('ctx', 'dp'), axis=0, tiled=True)  35.8 us
    transpose x2, local copies, waits for them, and re-layouts, arrange_rows(): shaped.transpose(0, 2, 3, 1, 4)  26 us
  transfers between devices with their start and end apart: 6, of which 4 were waited for; matrix products, arithmetic and copies ran while one was open for 13% of the time, Pallas kernels for 0%

commit v1 on v0

--- a/solution.py
+++ b/solution.py
@@ -220,7 +220,8 @@
         jnp.bfloat16
     )[None]
     scaled = grad_normed * norm_gain[None, :]
-    inner_sum = lax.psum(jnp.sum(hidden_f * scaled, axis=1), ("exp", "dp"))
+    field_in = jnp.sum(hidden_f * scaled, axis=1)
+    inner_sum = jnp.sum(lax.all_gather(field_in, ("exp", "dp")), axis=0)
     projection = (inner_sum / model_width)[:, None]
     grad_hidden = (
         out_grad.astype(jnp.float32) + inv_rms * scaled - hidden_f * inv_rms**3 * projection

time: 657 us -> 682 us (1.038)
  blocking collectives: 259 us -> 276 us
  waiting for transfers between devices: 179 us -> 187 us
    reduce_scatter x1, waiting for transfers between devices: 60.3 us -> 81 us  [per_device(): lax.psum_scatter(arrange_sums(full_out, ctx_count, dp_count, exp_count, c...]
    all_gather x0 -> x1, blocking collectives: none -> 17.4 us  [per_device(): inner_sum = jnp.sum(lax.all_gather(field_in, ('exp', 'dp')), axis=0)]
    reduce_scatter x1, waiting for transfers between devices: 81.2 us -> 70.1 us  [per_device(): lax.psum_scatter(arrange_sums(full_back, ctx_count, dp_count, exp_count,...]
    unnamed x55 -> x43, local copies, waits for them, and re-layouts: 19.4 us -> 17.2 us
  transfers between devices with their start and end apart: 6 -> 6, of which waited for: 4 -> 3; matrix products, arithmetic and copies ran while one was open for 13% -> 15% of each run, Pallas kernels for 0% -> 0%
where the time goes in v1:
time: 682 us; the launch traced here: 676 us
  blocking collectives  276 us (40%)
  waiting for transfers between devices  187 us (27%)
  local copies, waits for them, and re-layouts  113 us (17%)
  matrix products  38.9 us (6%)
  other arithmetic  30.4 us (4%)
  starting transfers between devices  15.3 us (2%)
  between operations  14.5 us (2%)
    reduce_scatter x1, waiting for transfers between devices, per_device(): lax.psum_scatter(arrange_sums(full_out, ctx_count, dp_count, exp_count, c...  81 us
    reduce_scatter x1, waiting for transfers between devices, per_device(): lax.psum_scatter(arrange_sums(full_back, ctx_count, dp_count, exp_count,...  70.1 us
    all_gather x2, blocking collectives, entering(): lax.all_gather(a.astype(kind), axis)  48.3 us
    psum x1, blocking collectives, per_device(): grad_probs = lax.psum(probs_part, ('exp', 'dp'))  45.8 us
    psum x1, blocking collectives, per_device(): lax.psum((keys_first + keys_second).astype(jnp.bfloat16), ('exp', 'dp'))  45.7 us
    psum x1, blocking collectives, per_device(): grad_gain = lax.psum(gain_part, 'ctx')  39 us
    all_gather x1, waiting for transfers between devices, per_device(): all_rows = lax.all_gather(got_rows, ('ctx', 'dp'), axis=0, tiled=True)  35.8 us
    transpose x2, local copies, waits for them, and re-layouts, arrange_rows(): shaped.transpose(0, 2, 3, 1, 4)  26 us
  transfers between devices with their start and end apart: 6, of which 3 were waited for; matrix products, arithmetic and copies ran while one was open for 15% of the time, Pallas kernels for 0%

profile of v1, /device:TPU:2, one launch (start us, length us, event | category | flops | bytes accessed | tf_op | source)
XLA Modules:
  0.0 675.5 jit_solution(13509943696238013684)
XLA Ops:
  7.3 0.9 copy.158
  9.5 0.8 copy.161
  10.4 0.9 broadcast_in_dim.74
  11.6 13.2 %scatter_fusion = bf16[8,40,256]{2,1,0:T(8,128)(2,1)S(1)} fusion(bf16[8,40,256]{2,1,0:T(8,128)(2,1)S(1)} %broadcast_in_dim.73.clone.1, s32[256]{0:T(256)S(1)} %bitcast.194, bf16[256,256]{1,0:T(8,128)(2,1)S(1)} %fusion.19), kind=kCustom, calls=%fused_computation.2 | custom fusion | bytes 395264 | tf_op jit(solution)/shard_map/scatter | solution.py:188
  24.9 18.0 %all_to_all.66 = bf16[8,40,1,256]{3,1,2,0:T(8,128)(2,1)S(1)} all-to-all(bf16[8,40,1,256]{3,1,2,0:T(8,128)(2,1)S(1)} %bitcast.201), channel_id=1, replica_groups=mesh['ctx'=16,'exp'=8,'dp'=2] {'exp'}, dimensions={0} | all-to-all | bytes 327680 | tf_op jit(solution)/shard_map/all_to_all | solution.py:189
  44.6 20.7 %all-gather.5 = bf16[16,1,4]{2,1,0:T(2,128)(2,1)S(1)} all-gather(bf16[1,1,4]{2,1,0:T(2,128)(2,1)S(1)} %get-tuple-element.297), channel_id=1, replica_groups=mesh['ctx'=16,'exp'=8,'dp'=2] {'ctx'}, dimensions={0}, use_global_device_ids=true | all-gather | bytes 136 | tf_op jit(solution)/shard_map/all_gather | solution.py:13
  65.4 1.0 copy.152
  67.0 27.6 %all-gather = bf16[64,64,64]{2,1,0:T(8,128)(2,1)} all-gather(bf16[4,64,64]{2,1,0:T(8,128)(2,1)S(1)} %convolution_convert_fusion.4), channel_id=2, replica_groups=mesh['ctx'=16,'exp'=8,'dp'=2] {'ctx'}, dimensions={0}, use_global_device_ids=true | all-gather | bytes 557056 | tf_op jit(solution)/shard_map/all_gather | solution.py:13
  94.8 1.0 while.26
  94.9 0.9 convert_add_fusion.4
  96.7 23.5 %psum.35 = f32[128]{0:T(128)S(1)} all-reduce(f32[128]{0:T(128)S(1)} %get-tuple-element.289), channel_id=1, replica_groups=mesh['ctx'=16,'exp'=8,'dp'=2] {'exp','dp'}, use_global_device_ids=true, to_apply=%region_4.5 | all-reduce | flops 128 | bytes 1024 | tf_op jit(solution)/shard_map/psum | solution.py:153
  121.1 13.2 %scatter_fusion.1 = bf16[8,40,256]{2,1,0:T(8,128)(2,1)S(1)} fusion(bf16[8,40,256]{2,1,0:T(8,128)(2,1)S(1)} %broadcast_in_dim.73.clone, s32[256]{0:T(256)S(1)} %bitcast.195, bf16[256,256]{1,0:T(8,128)(2,1)S(1)} %reshape.275), kind=kCustom, calls=%fused_computation.3 | custom fusion | bytes 395264 | tf_op jit(solution)/shard_map/scatter | solution.py:162
  134.3 12.5 %all_to_all.67 = bf16[8,40,1,256]{3,1,2,0:T(8,128)(2,1)S(1)} all-to-all(bf16[8,40,1,256]{3,1,2,0:T(8,128)(2,1)S(1)} %bitcast.200), channel_id=1, replica_groups=mesh['ctx'=16,'exp'=8,'dp'=2] {'exp'}, dimensions={0} | all-to-all | bytes 327680 | tf_op jit(solution)/shard_map/all_to_all | solution.py:163
  148.1 13.0 %copy.164 = bf16[16,40,8,2,256]{4,3,2,1,0:T(2,128)(2,1)} copy(bf16[16,40,8,2,256]{4,2,1,3,0:T(8,128)(2,1)} %bitcast.204) | data formatting | bytes 10485760 | tf_op jit(solution)/shard_map/transpose | solution.py:105
  161.1 9.6 %reshape.238 = bf16[640,4096]{1,0:T(8,128)(2,1)} reshape(bf16[16,40,8,2,256]{4,3,2,1,0:T(2,128)(2,1)} %copy.164) | data formatting | bytes 10485760 | tf_op jit(solution)/shard_map/reshape | solution.py:105
  170.7 35.8 %all-gather.12.cloned.1.call-done = bf16[32,40,8,1,256]{4,2,3,1,0:T(8,128)(2,1)} async-done(((bf16[1,40,8,1,256]{4,2,3,1,0:T(8,128)(2,1)}), bf16[32,40,8,1,256]{4,2,3,1,0:T(8,128)(2,1)}) %all-gather.12.cloned.1.call-update) | async-done | bytes 5242896 | tf_op jit(solution)/shard_map/all_gather | solution.py:164
  206.6 13.0 %copy.167 = bf16[16,40,8,2,256]{4,3,2,1,0:T(2,128)(2,1)} copy(bf16[16,40,8,2,256]{4,2,1,3,0:T(8,128)(2,1)} %bitcast.205) | data formatting | bytes 10485760 | tf_op jit(solution)/shard_map/transpose | solution.py:105
  219.6 9.6 %reshape.242 = bf16[640,4096]{1,0:T(8,128)(2,1)} reshape(bf16[16,40,8,2,256]{4,3,2,1,0:T(2,128)(2,1)} %copy.167) | data formatting | bytes 10485760 | tf_op jit(solution)/shard_map/reshape | solution.py:105
  229.2 4.2 fusion.10
  233.9 1.5 fusion.5
  235.5 2.4 multiply_convert_fusion
  238.0 1.6 fusion.3
  239.6 3.9 add_convert_fusion
  243.5 9.4 %convert_element_type.165 = bf16[16,40,8,2,256]{4,3,2,1,0:T(2,128)(2,1)} reshape(bf16[640,4096]{1,0:T(8,128)(2,1)} %add_convert_fusion) | data formatting | bytes 10485760 | tf_op jit(solution)/shard_map/convert_element_type | solution.py:201
  252.9 3.4 copy.168
  256.4 4.5 copy.189
  261.4 2.5 convert_bitcast_fusion
  263.9 2.3 copy.176
  266.3 4.6 copy.191
  271.0 5.9 fusion.2
  276.9 5.8 fusion
  282.7 70.1 %reduce-scatter.3.cloned.1.call-done = bf16[40,2048]{1,0:T(8,128)(2,1)} async-done(((bf16[1280,2048]{1,0:T(8,128)(2,1)}), bf16[40,2048]{1,0:T(8,128)(2,1)}) %reduce-scatter.3.cloned.1.call-update) | async-done | bytes 163856 | tf_op jit(solution)/shard_map/reduce_scatter | solution.py:200
  352.8 0.9 copy.190
  354.5 7.2 %all-to-all-start.2 = ((bf16[1,40,8,256]{3,1,0,2:T(8,128)(2,1)}), bf16[1,40,8,256]{3,1,0,2:T(8,128)(2,1)S(1)}, u32[]{:S(2)}, u32[]{:S(2)}) async-start(bf16[1,40,8,256]{3,1,0,2:T(8,128)(2,1)} %copy.169), calls=%async_computation.3 | async-start | bytes 327680 | tf_op jit(solution)/shard_map/all_to_all | solution.py:207
  361.7 5.7 fusion.1
  367.5 81.0 %reduce-scatter.5.cloned.1.call-done = bf16[40,2048]{1,0:T(8,128)(2,1)} async-done(((bf16[1280,2048]{1,0:T(8,128)(2,1)}), bf16[40,2048]{1,0:T(8,128)(2,1)}) %reduce-scatter.5.cloned.1.call-update) | async-done | bytes 163856 | tf_op jit(solution)/shard_map/reduce_scatter | solution.py:173
  448.5 0.9 copy.192
  450.1 7.0 %all-to-all-start.3 = ((bf16[1,40,8,256]{3,1,0,2:T(8,128)(2,1)}), bf16[1,40,8,256]{3,1,0,2:T(8,128)(2,1)S(1)}, u32[]{:S(2)}, u32[]{:S(2)}) async-start(bf16[1,40,8,256]{3,1,0,2:T(8,128)(2,1)} %copy.177), calls=%async_computation.5 | async-start | bytes 327680 | tf_op jit(solution)/shard_map/all_to_all | solution.py:180
  457.1 1.7 gather_fusion
  459.4 17.4 %all-gather.6 = f32[16,1,128]{2,1,0:T(1,128)S(1)} all-gather(f32[1,1,128]{2,1,0:T(1,128)S(1)} %bitcast.228), channel_id=5, replica_groups=mesh['ctx'=16,'exp'=8,'dp'=2] {'exp','dp'}, dimensions={0}, use_global_device_ids=true | all-gather | bytes 8704 | tf_op jit(solution)/shard_map/all_gather | solution.py:224
  478.3 25.5 %all-gather.4 = bf16[64,64,64]{2,1,0:T(8,128)(2,1)} all-gather(bf16[4,64,64]{2,1,0:T(8,128)(2,1)S(1)} %convolution_convert_fusion.3), channel_id=6, replica_groups=mesh['ctx'=16,'exp'=8,'dp'=2] {'ctx'}, dimensions={0}, use_global_device_ids=true | all-gather | bytes 557056 | tf_op jit(solution)/shard_map/all_gather | solution.py:35
  503.8 22.9 %while.27 = (s32[]{:T(128)}, f32[4,64,64]{2,1,0:T(8,128)S(1)}, s32[]{:T(128)}, bf16[16,4]{1,0:T(8,128)(2,1)}, bf16[16,4,64,64]{3,2,1,0:T(8,128)(2,1)}, /*index=5*/s32[]{:T(128)}, s32[]{:T(128)}, s32[]{:T(128)}, s32[]{:T(128)}) while((s32[]{:T(128)}, f32[4,64,64]{2,1,0:T(8,128)S(1)}, s32[]{:T(128)}, bf16[16,4]{1,0:T(8,128)(2,1)}, ...), condition=%wide.region_15.16_spmd, body=%wide.region_14.15_spmd.sunk | while | flops 49162 | bytes 164035 | solution.py:52
  504.5 0.9 convert_add_fusion.5
  506.1 0.9 convert_add_fusion.5
  507.8 0.9 convert_add_fusion.5
  509.4 0.9 convert_add_fusion.5
  511.1 0.9 convert_add_fusion.5
  512.7 0.9 convert_add_fusion.5
  514.3 0.9 convert_add_fusion.5
  516.0 0.9 convert_add_fusion.5
  517.6 0.9 convert_add_fusion.5
  519.3 0.9 convert_add_fusion.5
  520.9 0.9 convert_add_fusion.5
  522.5 0.9 convert_add_fusion.5
  524.2 0.9 convert_add_fusion.5
  525.8 0.9 convert_add_fusion.5
  527.1 1.7 gather_fusion.1
  529.0 45.8 %psum.38 = f32[128,2]{1,0:T(8,128)S(1)} all-reduce(f32[128,2]{1,0:T(8,128)S(1)} %reshape.249), channel_id=1, replica_groups=mesh['ctx'=16,'exp'=8,'dp'=2] {'exp','dp'}, use_global_device_ids=true, to_apply=%region_28.29 | all-reduce | flops 256 | bytes 2048 | tf_op jit(solution)/shard_map/psum | solution.py:187
  575.4 39.0 %psum.39 = f32[256]{0:T(256)} all-reduce(f32[256]{0:T(256)S(1)} %get-tuple-element.263), channel_id=1, replica_groups=mesh['ctx'=16,'exp'=8,'dp'=2] {'ctx'}, use_global_device_ids=true, to_apply=%region_30.31 | all-reduce | flops 256 | bytes 2048 | tf_op jit(solution)/shard_map/psum | solution.py:230
  614.4 1.4 fusion.26
  616.7 1.3 fusion.14
  618.7 45.7 %all-reduce.1 = (bf16[128,64]{0,1:T(8,128)(2,1)S(1)}, bf16[128,64]{0,1:T(8,128)(2,1)S(1)}) all-reduce(bf16[128,64]{0,1:T(8,128)(2,1)S(1)} %fusion.16, bf16[128,64]{0,1:T(8,128)(2,1)S(1)} %fusion.17), channel_id=1, replica_groups=mesh['ctx'=16,'exp'=8,'dp'=2] {'exp','dp'}, use_global_device_ids=true, to_apply=%region_17.18 | all-reduce | flops 16384 | bytes 65536 | tf_op jit(solution)/shard_map/psum | solution.py:237
  665.9 1.1 reduce_window_sum.47
  667.0 1.1 reduce_window_sum.48
  (129 shorter events, 26.4 us)
Async XLA Ops:
  7.2 222.0 %copy-start = (bf16[1,4096,256]{2,1,0:T(8,128)(2,1)S(1)}, bf16[1,4096,256]{2,1,0:T(8,128)(2,1)}, u32[]{:S(2)}) copy-start(bf16[1,4096,256]{2,1,0:T(8,128)(2,1)} %param.26) | copy-start | bytes 6291460
  7.2 59.6 %copy-start.9 = (bf16[128,64]{0,1:T(8,128)(2,1)S(1)}, bf16[128,64]{0,1:T(8,128)(2,1)}, u32[]{:S(2)}) copy-start(bf16[128,64]{0,1:T(8,128)(2,1)} %param.18) | copy-start | bytes 49156
  7.2 87.4 %copy-start.8 = (bf16[128,64]{0,1:T(8,128)(2,1)S(1)}, bf16[128,64]{0,1:T(8,128)(2,1)}, u32[]{:S(2)}) copy-start(bf16[128,64]{0,1:T(8,128)(2,1)} %param.19) | copy-start | bytes 49156
  7.2 89.4 %copy-start.11 = (bf16[128,256]{1,0:T(8,128)(2,1)S(1)}, bf16[128,256]{1,0:T(8,128)(2,1)}, u32[]{:S(2)}) copy-start(bf16[128,256]{1,0:T(8,128)(2,1)} %param.16) | copy-start | bytes 196612
  7.2 113.6 %copy-start.12 = (f32[256]{0:T(256)S(1)}, f32[256]{0:T(256)}, u32[]{:S(2)}) copy-start(f32[256]{0:T(256)} %param.23) | copy-start | bytes 3076
  7.2 140.9 %all-gather.10.cloned.1.call-start = ((), (), s32[]{:S(2)}) async-start(), calls=%async_computation.8 | async-start | bytes 5406720 | tf_op jit(solution)/shard_map/all_gather | solution.py:190
  43.6 162.9 %all-gather.12.cloned.1.call-start = ((), (), s32[]{:S(2)}) async-start(), calls=%async_computation.9 | async-start | bytes 5406720 | tf_op jit(solution)/shard_map/all_gather | solution.py:164
  66.4 67.9 %copy-start.14 = (f32[4,128]{1,0:T(4,128)}, f32[4,128]{1,0:T(4,128)S(1)}, u32[]{:S(2)}) copy-start(f32[4,128]{1,0:T(4,128)S(1)} %copy.150) | copy-start | bytes 6148
  94.8 66.3 %copy-start.10 = (f32[128,128]{1,0:T(8,128)}, f32[128,128]{1,0:T(8,128)S(1)}, u32[]{:S(2)}) copy-start(f32[128,128]{1,0:T(8,128)S(1)} %fusion.65) | copy-start | bytes 196612
  95.8 38.5 %copy-start.13 = (bf16[16,4]{1,0:T(8,128)(2,1)}, bf16[16,4]{1,0:T(8,128)(2,1)S(1)}, u32[]{:S(2)}) copy-start(bf16[16,4]{1,0:T(8,128)(2,1)S(1)} %get-tuple-element.435) | copy-start | bytes 388
  147.5 205.4 %reduce-scatter.3.cloned.1.call-start = ((), (), s32[]{:S(2)}) async-start(), calls=%async_computation.6 | async-start | bytes 5406720 | tf_op jit(solution)/shard_map/reduce_scatter | solution.py:200
  229.2 4.2 copy-start.1
  229.2 4.7 copy-start.2
  233.9 1.6 copy-start.3
  238.0 1.6 copy-start.4
  238.0 1.6 copy-start.6
  260.9 187.6 %reduce-scatter.5.cloned.1.call-start = ((), (), s32[]{:S(2)}) async-start(), calls=%async_computation.7 | async-start | bytes 5406720 | tf_op jit(solution)/shard_map/reduce_scatter | solution.py:173
  270.9 5.9 copy-start.5
  354.5 95.7 %all-to-all-start.2 = ((bf16[1,40,8,256]{3,1,0,2:T(8,128)(2,1)}), bf16[1,40,8,256]{3,1,0,2:T(8,128)(2,1)S(1)}, u32[]{:S(2)}, u32[]{:S(2)}) async-start(bf16[1,40,8,256]{3,1,0,2:T(8,128)(2,1)} %copy.169), calls=%async_computation.3 | async-start | bytes 327680 | tf_op jit(solution)/shard_map/all_to_all | solution.py:207
  361.7 115.1 %copy-start.7 = (bf16[128,256]{1,0:T(8,128)(2,1)S(1)}, bf16[128,256]{1,0:T(8,128)(2,1)}, u32[]{:S(2)}) copy-start(bf16[128,256]{1,0:T(8,128)(2,1)} %param.27) | copy-start | bytes 196612
  361.7 115.1 %copy-start.15 = (f32[128]{0:T(128)S(1)}, f32[128]{0:T(128)}, u32[]{:S(2)}) copy-start(f32[128]{0:T(128)} %get-tuple-element.298) | copy-start | bytes 1540
  450.1 76.9 %all-to-all-start.3 = ((bf16[1,40,8,256]{3,1,0,2:T(8,128)(2,1)}), bf16[1,40,8,256]{3,1,0,2:T(8,128)(2,1)S(1)}, u32[]{:S(2)}, u32[]{:S(2)}) async-start(bf16[1,40,8,256]{3,1,0,2:T(8,128)(2,1)} %copy.177), calls=%async_computation.5 | async-start | bytes 327680 | tf_op jit(solution)/shard_map/all_to_all | solution.py:180
Sparse Core Ops, SparseCore 0:
  43.7 49.1 all-gather.9
  147.6 58.8 all-gather.11
  261.0 91.7 reduce-scatter.2
  356.7 91.7 reduce-scatter.4
